TPU v7x, 32 devices: a whole 2x2x4 slice. The times are simulated.
32 devices in a mesh: grp: 8 (over y, x, core), blk: 4 (over z).
Axes of the slice: x: 2, y: 2, z: 4, core: 2. Of those that a mesh axis runs over, the one named last changes fastest.
Arguments:
- gradient: bfloat16 [2048, 4096], P(('grp', 'blk')), may hold values from -6 to 6
- stats_left: float32 [32, 512, 512], P(('grp', 'blk')), as said below
- stats_right: float32 [32, 512, 512], P(('grp', 'blk')), as said below
- root_left: bfloat16 [32, 512, 512], P(('grp', 'blk')), may hold values from -0.25 to 0.25
- root_right: bfloat16 [32, 512, 512], P(('grp', 'blk')), may hold values from -0.25 to 0.25
- slot_block: int32 [8, 4], replicated, may hold values from 0 to 3, each once within a row
- refresh_slots: int32 [4], replicated, may hold values from 0 to 31, as said below
- newton_steps: int32 [4], replicated, may hold values from 1 to 3, as said below
Outputs:
- new_left: float32 [32, 512, 512], P(('grp', 'blk'))
- new_right: float32 [32, 512, 512], P(('grp', 'blk'))
- new_root_left: bfloat16 [32, 512, 512], P(('grp', 'blk'))
- new_root_right: bfloat16 [32, 512, 512], P(('grp', 'blk'))
- update: bfloat16 [2048, 4096], P(('grp', 'blk'))
Inputs may be any that keep to these rules, and one draw needn't show every extreme that they name: `stats_left`: each matrix is symmetric positive definite. `stats_right`: each matrix is symmetric positive definite. `slot_block`: row c lists each block row once. `refresh_slots`: distinct slot numbers. `newton_steps`: not all elements are equal.
All inputs are finite; a program needn't handle non-finite values.
Results may differ from a plain program's by a relative error of at most 0.0051.
Values may be sent and summed in bfloat16 or wider, within the bound.
A program may use at most 64 MiB of HBM per device.

v0:
```python
import jax
import jax.numpy as jnp
from jax import lax
from jax.sharding import PartitionSpec as P

B = 512


damping = 0.0001
decay_rate = 0.9
root_order = 4.0


def batch_product(left, right):
    return jnp.einsum(
        "kij,kjl->kil",
        left,
        right,
        precision=lax.Precision.HIGHEST,
        preferred_element_type=jnp.float32,
    )


def inverse_roots(statistics, step_count):
    identity_matrix = jnp.eye(statistics.shape[1], dtype=jnp.float32)
    shifted = statistics + damping * identity_matrix
    frobenius = jnp.sqrt(jnp.sum(shifted * shifted, axis=(1, 2), keepdims=True))
    scaling = (1.0 + root_order) / (2.0 * frobenius)
    iterate = scaling ** (1.0 / root_order) * identity_matrix
    moving = scaling * shifted

    def newton(unused, state_pair):
        iterate, moving = state_pair
        factor = ((root_order + 1.0) * identity_matrix - moving) / root_order
        iterate = batch_product(iterate, factor)
        factor_sq = batch_product(factor, factor)
        moving = batch_product(batch_product(factor_sq, factor_sq), moving)
        return (iterate, moving)

    return lax.fori_loop(0, step_count, newton, (iterate, moving))[0]


def steps_for(slot_number, refresh_slots, newton_steps):
    return jnp.sum(jnp.where(refresh_slots == slot_number, newton_steps, 0))


def per_device(
    gradient,
    stats_left,
    stats_right,
    root_left,
    root_right,
    slot_block,
    refresh_slots,
    newton_steps,
):
    groups = lax.axis_size("grp")
    owners = lax.axis_size("blk")
    rows_dev = gradient.shape[0]
    group_share = groups // owners
    group_id = lax.axis_index("grp")
    owner_id = lax.axis_index("blk")
    slot_order = lax.dynamic_index_in_dim(slot_block, group_id, 0, keepdims=False)
    gathered = lax.all_to_all(gradient, "grp", split_axis=1, concat_axis=0, tiled=True)
    by_row = gathered.reshape(owners, group_share * rows_dev, B)
    arranged = jnp.take(by_row, slot_order, axis=0)
    received = lax.all_to_all(arranged, "blk", split_axis=0, concat_axis=1, tiled=True)
    grad_block = (
        received.reshape(owners, group_share, rows_dev, B).transpose(1, 0, 2, 3).reshape(B, B)
    )
    gram_weight = (1.0 - decay_rate) / B
    left_new = decay_rate * stats_left[0] + gram_weight * jnp.dot(
        grad_block, grad_block.T, preferred_element_type=jnp.float32
    )
    right_new = decay_rate * stats_right[0] + gram_weight * jnp.dot(
        grad_block.T, grad_block, preferred_element_type=jnp.float32
    )
    my_slot = group_id * owners + owner_id
    steps_mine = steps_for(my_slot, refresh_slots, newton_steps)
    refresh_mine = steps_mine > 0
    stacked = inverse_roots(jnp.stack([left_new, right_new]), steps_mine)
    left_root = jnp.where(refresh_mine, stacked[0].astype(jnp.bfloat16), root_left[0])
    right_root = jnp.where(refresh_mine, stacked[1].astype(jnp.bfloat16), root_right[0])
    half_product = jnp.dot(grad_block, right_root, preferred_element_type=jnp.float32).astype(
        jnp.bfloat16
    )
    precon = jnp.dot(left_root, half_product, preferred_element_type=jnp.float32)
    grad_wide = grad_block.astype(jnp.float32)
    graft_ratio = jnp.sqrt(jnp.mean(grad_wide * grad_wide)) / jnp.sqrt(
        jnp.mean(precon * precon) + 1e-06
    )
    update_block = (precon * graft_ratio).astype(jnp.bfloat16)
    pieces = update_block.reshape(group_share, owners, rows_dev, B).transpose(1, 0, 2, 3)
    pieces = pieces.reshape(owners, group_share * rows_dev, B)
    returned_rows = lax.all_to_all(pieces, "blk", split_axis=0, concat_axis=0, tiled=True)
    positions = jnp.arange(owners, dtype=jnp.int32)
    matches = slot_order[None, :] == positions[:, None]
    inverse = jnp.sum(jnp.where(matches, positions[None, :], 0), axis=1)
    ordered = jnp.take(returned_rows, inverse, axis=0).reshape(groups * rows_dev, B)
    update_rows = lax.all_to_all(ordered, "grp", split_axis=0, concat_axis=1, tiled=True)
    return (left_new[None], right_new[None], left_root[None], right_root[None], update_rows)


def solution(mesh):
    placed = (
        P(("grp", "blk"), None),
        P(("grp", "blk"), None, None),
        P(("grp", "blk"), None, None),
        P(("grp", "blk"), None, None),
        P(("grp", "blk"), None, None),
        P(),
        P(),
        P(),
    )
    return jax.shard_map(
        per_device,
        mesh=mesh,
        in_specs=placed,
        out_specs=(
            P(("grp", "blk"), None, None),
            P(("grp", "blk"), None, None),
            P(("grp", "blk"), None, None),
            P(("grp", "blk"), None, None),
            P(("grp", "blk"), None),
        ),
        check_vma=False,
    )
```

profile of v0, /device:TPU:0, one launch (start us, length us, event | category | flops | bytes accessed | tf_op | source)
XLA Modules:
  0.0 131.8 jit_solution(17497153416736444944)
XLA Ops:
  0.6 1.9 %copy.63 = bf16[8,8,8,512]{3,2,0,1:T(8,128)(2,1)} copy(bf16[8,8,8,512]{3,2,1,0:T(8,128)(2,1)} %bitcast.82) | data formatting | bytes 1048576 | tf_op jit(solution)/shard_map/all_to_all | solution.py:64
  2.5 5.2 %all-to-all-start = ((bf16[64,8,512]{2,0,1:T(8,128)(2,1)}), bf16[64,8,512]{2,0,1:T(8,128)(2,1)S(1)}, u32[]{:S(2)}, u32[]{:S(2)}) async-start(bf16[64,8,512]{2,0,1:T(8,128)(2,1)} %bitcast.60), calls=%async_computation | async-start | bytes 1048576 | tf_op jit(solution)/shard_map/all_to_all | solution.py:64
  8.0 9.5 %all-to-all-done = bf16[64,8,512]{2,0,1:T(8,128)(2,1)S(1)} async-done(((bf16[64,8,512]{2,0,1:T(8,128)(2,1)}), bf16[64,8,512]{2,0,1:T(8,128)(2,1)S(1)}, u32[]{:S(2)}, u32[]{:S(2)}) %all-to-all-start) | async-done | bytes 524320 | tf_op jit(solution)/shard_map/all_to_all | solution.py:64
  18.0 0.9 broadcast_select_fusion.1
  18.9 5.0 %all-to-all-start.1 = ((bf16[4,128,512]{2,1,0:T(8,128)(2,1)}), bf16[4,128,512]{2,1,0:T(8,128)(2,1)S(1)}, u32[]{:S(2)}, u32[]{:S(2)}) async-start(bf16[4,128,512]{2,1,0:T(8,128)(2,1)} %broadcast_select_fusion.1), calls=%async_computation.1 | async-start | bytes 1048576 | tf_op jit(solution)/shard_map/all_to_all | solution.py:67
  24.1 1.3 %copy.47 = f32[512,512]{0,1:T(8,128)} copy(f32[512,512]{1,0:T(8,128)S(1)} %fusion.19) | data formatting | bytes 2097152 | tf_op jit(solution)/shard_map/convert_element_type | solution.py:25
  26.8 9.4 %all-to-all-done.1 = bf16[4,128,512]{2,1,0:T(8,128)(2,1)S(1)} async-done(((bf16[4,128,512]{2,1,0:T(8,128)(2,1)}), bf16[4,128,512]{2,1,0:T(8,128)(2,1)S(1)}, u32[]{:S(2)}, u32[]{:S(2)}) %all-to-all-start.1) | async-done | bytes 524320 | tf_op jit(solution)/shard_map/all_to_all | solution.py:67
  36.2 0.8 multiply_reduce_fusion.2
  39.3 1.8 %fusion.12 = f32[2,512,512]{2,1,0:T(8,128)} fusion(f32[1,512,512]{2,1,0:T(8,128)S(1)} %fusion.15, f32[1,512,512]{2,1,0:T(8,128)S(1)} %fusion.17, f32[2]{0:T(128)S(1)} %get-tuple-element.55, f32[512,512]{1,0:T(8,128)S(1)} %fusion.20), kind=kLoop, calls=%fused_computation.17 | loop fusion | flops 1572864 | bytes 5242888 | tf_op jit(solution)/shard_map/mul | solution.py:30
  41.5 56.3 %while.13 = (s32[]{:T(128)}, f32[2,512,512]{1,2,0:T(8,128)S(1)}, f32[2,512,512]{2,1,0:T(8,128)}, s32[]{:T(128)}, s32[]{:T(128)}) while((s32[]{:T(128)}, f32[2,512,512]{1,2,0:T(8,128)S(1)}, f32[2,512,512]{2,1,0:T(8,128)}, s32[]{:T(128)}, s32[]{:T(128)}) %tuple.29), condition=%wide.region_3.5_spmd.clone, body=%wide.region_2.4_spmd.clone.sunk | while | flops 12887523328 | bytes 32505916 | solution.py:40
  42.3 1.6 %copy.77 = f32[2,512,512]{2,1,0:T(8,128)S(1)} copy(f32[2,512,512]{2,1,0:T(8,128)} %get-tuple-element.93) | data formatting | bytes 4194304 | tf_op jit(solution)/shard_map/while
  44.2 3.7 %fusion.57 = f32[2,512,512]{1,2,0:T(8,128)S(1)} fusion(f32[2,512,512]{1,2,0:T(8,128)S(1)} %copy.76, f32[2,512,512]{2,1,0:T(8,128)S(1)} %copy.77, f32[512,512]{1,0:T(8,128)S(1)} %fusion.56), kind=kOutput, calls=%fused_computation.6.clone.1 | convolution fusion | flops 3222274048 | bytes 7340032 | tf_op jit(solution)/shard_map/while/body/kij,kjl->kil/dot_general | solution.py:15
  47.9 3.8 %fusion.58 = f32[2,512,512]{2,1,0:T(8,128)S(1)} fusion(f32[2,512,512]{2,1,0:T(8,128)S(1)} %copy.77, f32[512,512]{1,0:T(8,128)S(1)} %fusion.56), kind=kOutput, calls=%fused_computation.4.clone.1 | convolution fusion | flops 3222274048 | bytes 5242880 | tf_op jit(solution)/shard_map/while/body/kij,kjl->kil/dot_general | solution.py:15
  51.7 3.5 %fusion.59 = f32[2,512,512]{2,1,0:T(8,128)S(1)} fusion(f32[2,512,512]{2,1,0:T(8,128)S(1)} %fusion.58), kind=kOutput, calls=%fused_computation.58.clone.1 | convolution fusion | flops 3221225472 | bytes 4194304 | tf_op jit(solution)/shard_map/while/body/kij,kjl->kil/dot_general | solution.py:15
  55.2 4.9 %fusion.60 = f32[2,512,512]{2,1,0:T(8,128)} fusion(f32[2,512,512]{2,1,0:T(8,128)S(1)} %fusion.59, f32[2,512,512]{2,1,0:T(8,128)S(1)} %copy.77), kind=kOutput, calls=%fused_computation.59.clone.1 | convolution fusion | flops 3221225472 | bytes 6291456 | tf_op jit(solution)/shard_map/while/body/kij,kjl->kil/dot_general | solution.py:15
  60.7 1.6 %copy.77 = f32[2,512,512]{2,1,0:T(8,128)S(1)} copy(f32[2,512,512]{2,1,0:T(8,128)} %get-tuple-element.93) | data formatting | bytes 4194304 | tf_op jit(solution)/shard_map/while
  62.6 3.7 %fusion.57 = f32[2,512,512]{1,2,0:T(8,128)S(1)} fusion(f32[2,512,512]{1,2,0:T(8,128)S(1)} %copy.76, f32[2,512,512]{2,1,0:T(8,128)S(1)} %copy.77, f32[512,512]{1,0:T(8,128)S(1)} %fusion.56), kind=kOutput, calls=%fused_computation.6.clone.1 | convolution fusion | flops 3222274048 | bytes 7340032 | tf_op jit(solution)/shard_map/while/body/kij,kjl->kil/dot_general | solution.py:15
  66.3 3.8 %fusion.58 = f32[2,512,512]{2,1,0:T(8,128)S(1)} fusion(f32[2,512,512]{2,1,0:T(8,128)S(1)} %copy.77, f32[512,512]{1,0:T(8,128)S(1)} %fusion.56), kind=kOutput, calls=%fused_computation.4.clone.1 | convolution fusion | flops 3222274048 | bytes 5242880 | tf_op jit(solution)/shard_map/while/body/kij,kjl->kil/dot_general | solution.py:15
  70.1 3.5 %fusion.59 = f32[2,512,512]{2,1,0:T(8,128)S(1)} fusion(f32[2,512,512]{2,1,0:T(8,128)S(1)} %fusion.58), kind=kOutput, calls=%fused_computation.58.clone.1 | convolution fusion | flops 3221225472 | bytes 4194304 | tf_op jit(solution)/shard_map/while/body/kij,kjl->kil/dot_general | solution.py:15
  73.6 4.9 %fusion.60 = f32[2,512,512]{2,1,0:T(8,128)} fusion(f32[2,512,512]{2,1,0:T(8,128)S(1)} %fusion.59, f32[2,512,512]{2,1,0:T(8,128)S(1)} %copy.77), kind=kOutput, calls=%fused_computation.59.clone.1 | convolution fusion | flops 3221225472 | bytes 6291456 | tf_op jit(solution)/shard_map/while/body/kij,kjl->kil/dot_general | solution.py:15
  79.1 1.6 %copy.77 = f32[2,512,512]{2,1,0:T(8,128)S(1)} copy(f32[2,512,512]{2,1,0:T(8,128)} %get-tuple-element.93) | data formatting | bytes 4194304 | tf_op jit(solution)/shard_map/while
  81.0 3.7 %fusion.57 = f32[2,512,512]{1,2,0:T(8,128)S(1)} fusion(f32[2,512,512]{1,2,0:T(8,128)S(1)} %copy.76, f32[2,512,512]{2,1,0:T(8,128)S(1)} %copy.77, f32[512,512]{1,0:T(8,128)S(1)} %fusion.56), kind=kOutput, calls=%fused_computation.6.clone.1 | convolution fusion | flops 3222274048 | bytes 7340032 | tf_op jit(solution)/shard_map/while/body/kij,kjl->kil/dot_general | solution.py:15
  84.7 3.8 %fusion.58 = f32[2,512,512]{2,1,0:T(8,128)S(1)} fusion(f32[2,512,512]{2,1,0:T(8,128)S(1)} %copy.77, f32[512,512]{1,0:T(8,128)S(1)} %fusion.56), kind=kOutput, calls=%fused_computation.4.clone.1 | convolution fusion | flops 3222274048 | bytes 5242880 | tf_op jit(solution)/shard_map/while/body/kij,kjl->kil/dot_general | solution.py:15
  88.5 3.5 %fusion.59 = f32[2,512,512]{2,1,0:T(8,128)S(1)} fusion(f32[2,512,512]{2,1,0:T(8,128)S(1)} %fusion.58), kind=kOutput, calls=%fused_computation.58.clone.1 | convolution fusion | flops 3221225472 | bytes 4194304 | tf_op jit(solution)/shard_map/while/body/kij,kjl->kil/dot_general | solution.py:15
  92.0 4.9 %fusion.60 = f32[2,512,512]{2,1,0:T(8,128)} fusion(f32[2,512,512]{2,1,0:T(8,128)S(1)} %fusion.59, f32[2,512,512]{2,1,0:T(8,128)S(1)} %copy.77), kind=kOutput, calls=%fused_computation.59.clone.1 | convolution fusion | flops 3221225472 | bytes 6291456 | tf_op jit(solution)/shard_map/while/body/kij,kjl->kil/dot_general | solution.py:15
  98.4 1.0 fusion.22
  99.4 2.7 %multiply_reduce_fusion.1 = (f32[]{:T(128)}, f32[512,512]{1,0:T(8,128)S(1)}) fusion(bf16[512,512]{1,0:T(8,128)(2,1)S(1)} %bitcast.74, bf16[1,512,512]{2,1,0:T(8,128)(2,1)S(1)} %get-tuple-element.56, bf16[1,512,512]{2,1,0:T(8,128)(2,1)} %get-tuple-element.57), kind=kOutput, calls=%fused_computation.30 | convolution fusion | flops 537657344 | bytes 2621444 | tf_op jit(solution)/shard_map/dot_general | solution.py:87
  103.6 0.8 copy.50
  104.4 3.5 %all-to-all-start.2 = ((bf16[4,128,512]{2,1,0:T(8,128)(2,1)}), bf16[4,128,512]{2,1,0:T(8,128)(2,1)S(1)}, u32[]{:S(2)}, u32[]{:S(2)}) async-start(bf16[4,128,512]{2,1,0:T(8,128)(2,1)} %bitcast.16), calls=%async_computation.2 | async-start | bytes 1048576 | tf_op jit(solution)/shard_map/all_to_all | solution.py:95
  108.0 10.1 %all-to-all-done.2 = bf16[4,128,512]{2,1,0:T(8,128)(2,1)S(1)} async-done(((bf16[4,128,512]{2,1,0:T(8,128)(2,1)}), bf16[4,128,512]{2,1,0:T(8,128)(2,1)S(1)}, u32[]{:S(2)}, u32[]{:S(2)}) %all-to-all-start.2) | async-done | bytes 524320 | tf_op jit(solution)/shard_map/all_to_all | solution.py:95
  118.8 12.1 %all_to_all.49 = bf16[8,64,512]{2,1,0:T(8,128)(2,1)S(1)} all-to-all(bf16[8,64,512]{2,1,0:T(8,128)(2,1)S(1)} %bitcast.80), channel_id=1, replica_groups=mesh['grp'=8,'blk'=4] {'grp'}, dimensions={0} | all-to-all | bytes 1048576 | tf_op jit(solution)/shard_map/all_to_all | solution.py:100
  131.0 0.8 copy.56
  (50 shorter events, 6.6 us)
Async XLA Ops:
  0.6 7.1 %copy-start = (s32[8,4]{0,1:T(4,128)S(1)}, s32[8,4]{0,1:T(4,128)}, u32[]{:S(2)}) copy-start(s32[8,4]{0,1:T(4,128)} %param.17) | copy-start | bytes 388
  2.5 14.9 %all-to-all-start = ((bf16[64,8,512]{2,0,1:T(8,128)(2,1)}), bf16[64,8,512]{2,0,1:T(8,128)(2,1)S(1)}, u32[]{:S(2)}, u32[]{:S(2)}) async-start(bf16[64,8,512]{2,0,1:T(8,128)(2,1)} %bitcast.60), calls=%async_computation | async-start | bytes 1048576 | tf_op jit(solution)/shard_map/all_to_all | solution.py:64
  18.9 6.5 %copy-start.8 = (s32[4]{0:T(128)S(1)}, s32[4]{0:T(128)}, u32[]{:S(2)}) copy-start(s32[4]{0:T(128)} %param.19) | copy-start | bytes 52
  18.9 6.5 %copy-start.9 = (s32[4]{0:T(128)S(1)}, s32[4]{0:T(128)}, u32[]{:S(2)}) copy-start(s32[4]{0:T(128)} %param.18) | copy-start | bytes 52
  18.9 17.2 %all-to-all-start.1 = ((bf16[4,128,512]{2,1,0:T(8,128)(2,1)}), bf16[4,128,512]{2,1,0:T(8,128)(2,1)S(1)}, u32[]{:S(2)}, u32[]{:S(2)}) async-start(bf16[4,128,512]{2,1,0:T(8,128)(2,1)} %broadcast_select_fusion.1), calls=%async_computation.1 | async-start | bytes 1048576 | tf_op jit(solution)/shard_map/all_to_all | solution.py:67
  24.1 13.0 %copy-start.10 = (f32[1,512,512]{2,1,0:T(8,128)S(1)}, f32[1,512,512]{2,1,0:T(8,128)}, u32[]{:S(2)}) copy-start(f32[1,512,512]{2,1,0:T(8,128)} %param.14) | copy-start | bytes 3145732
  36.2 1.4 %copy-start.2 = (bf16[4,2,64,512]{3,2,0,1:T(8,128)(2,1)}, bf16[4,2,64,512]{3,2,0,1:T(8,128)(2,1)S(1)}, u32[]{:S(2)}) copy-start(bf16[4,2,64,512]{3,2,0,1:T(8,128)(2,1)S(1)} %copy.46) | copy-start | bytes 1572868
  37.1 1.2 copy-start.6
  37.6 1.7 %copy-start.5 = (f32[1,512,512]{2,1,0:T(8,128)}, f32[1,512,512]{2,1,0:T(8,128)S(1)}, u32[]{:S(2)}) copy-start(f32[1,512,512]{2,1,0:T(8,128)S(1)} %fusion.15) | copy-start | bytes 3145732
  38.8 2.4 %copy-start.1 = (f32[1,512,512]{2,1,0:T(8,128)}, f32[1,512,512]{2,1,0:T(8,128)S(1)}, u32[]{:S(2)}) copy-start(f32[1,512,512]{2,1,0:T(8,128)S(1)} %fusion.17) | copy-start | bytes 3145732
  39.3 1.9 %copy-start.4 = (f32[512,512]{0,1:T(8,128)S(1)}, f32[512,512]{0,1:T(8,128)}, u32[]{:S(2)}) copy-start(f32[512,512]{0,1:T(8,128)} %copy.47) | copy-start | bytes 3145732
  98.4 1.0 copy-start.3
  99.4 4.2 %copy-start.7 = (bf16[1,512,512]{2,1,0:T(8,128)(2,1)}, bf16[1,512,512]{2,1,0:T(8,128)(2,1)S(1)}, u32[]{:S(2)}) copy-start(bf16[1,512,512]{2,1,0:T(8,128)(2,1)S(1)} %get-tuple-element.56) | copy-start | bytes 1572868
  104.4 13.7 %all-to-all-start.2 = ((bf16[4,128,512]{2,1,0:T(8,128)(2,1)}), bf16[4,128,512]{2,1,0:T(8,128)(2,1)S(1)}, u32[]{:S(2)}, u32[]{:S(2)}) async-start(bf16[4,128,512]{2,1,0:T(8,128)(2,1)} %bitcast.16), calls=%async_computation.2 | async-start | bytes 1048576 | tf_op jit(solution)/shard_map/all_to_all | solution.py:95
where the time goes:
time: 132 us
  matrix products  51.2 us (39%)
  waiting for transfers between devices  29 us (22%)
  starting transfers between devices  13.7 us (10%)
  local copies, waits for them, and re-layouts  13 us (10%)
  blocking collectives  12.1 us (9%)
  other arithmetic  6.97 us (5%)
  loops' own time  3.16 us (2%)
  between operations  2.78 us (2%)
    dot_general x12, matrix products, batch_product(): jnp.einsum('kij,kjl->kil', left, right, precision=lax.Precision.HIGHEST,...  47.5 us
    all_to_all x1, blocking collectives, per_device(): lax.all_to_all(ordered, 'grp', split_axis=0, concat_axis=1, tiled=True)  12.1 us
    all_to_all x1, waiting for transfers between devices, per_device(): lax.all_to_all(pieces, 'blk', split_axis=0, concat_axis=0, tiled=True)  10.1 us
    all_to_all x1, waiting for transfers between devices, per_device(): lax.all_to_all(gradient, 'grp', split_axis=1, concat_axis=0, tiled=True)  9.49 us
    all_to_all x1, waiting for transfers between devices, per_device(): lax.all_to_all(arranged, 'blk', split_axis=0, concat_axis=1, tiled=True)  9.36 us
    while x6, local copies, waits for them, and re-layouts  5.29 us
    all_to_all x1, starting transfers between devices, per_device(): lax.all_to_all(gradient, 'grp', split_axis=1, concat_axis=0, tiled=True)  5.2 us
    all_to_all x1, starting transfers between devices, per_device(): lax.all_to_all(arranged, 'blk', split_axis=0, concat_axis=1, tiled=True)  5 us
  transfers between devices with their start and end apart: 3, of which 3 were waited for; matrix products, arithmetic and copies ran while one was open for 2% of the time, Pallas kernels for 0%

commit v1 on v0

v1 whole, which is shorter than its diff:
```python
import functools

import jax
import jax.numpy as jnp
from jax import lax
from jax.experimental import pallas as pl
from jax.experimental.pallas import tpu as pltpu
from jax.sharding import PartitionSpec as P

damping = 0.0001
decay_rate = 0.9
root_order = 4.0
CHUNKS = 2
MESH = pl.DeviceIdType.MESH
F32 = jnp.float32
BF16 = jnp.bfloat16


def enter(groups, owners, grp, blk):
    barrier = pltpu.get_barrier_semaphore()
    for step in range(1, groups):
        peer = lax.rem(grp + step, groups)
        pl.semaphore_signal(barrier, inc=1, device_id=(peer, blk), device_id_type=MESH)
    for step in range(1, owners):
        peer = lax.rem(blk + step, owners)
        pl.semaphore_signal(barrier, inc=1, device_id=(grp, peer), device_id_type=MESH)
    pl.semaphore_wait(barrier, groups + owners - 2)


def remote(src, dst, send, recv, device):
    return pltpu.make_async_remote_copy(
        src_ref=src,
        dst_ref=dst,
        send_sem=send,
        recv_sem=recv,
        device_id=device,
        device_id_type=MESH,
    )


def inbound(groups, owners, order, x, g, landed, staged, local1, local2, s1, r1, s2, r2):
    grp, blk = lax.axis_index("grp"), lax.axis_index("blk")
    share = groups // owners
    block = landed[0].shape[-1] * CHUNKS
    width = landed[0].shape[-1]

    def columns(owner, chunk):
        return pl.ds(pl.multiple_of(owner * block + chunk * width, width), width)

    mine = []
    for chunk in range(CHUNKS):
        copy = pltpu.make_async_copy(
            x.at[:, columns(grp, chunk)], landed[chunk].at[grp], local1.at[chunk]
        )
        copy.start()
        mine.append(copy)
    enter(groups, owners, grp, blk)
    first = []
    for chunk in range(CHUNKS):
        row = []
        for step in range(1, groups):
            peer = lax.rem(grp + step, groups)
            copy = remote(
                x.at[:, columns(peer, chunk)],
                landed[chunk].at[grp],
                s1.at[chunk, step],
                r1.at[chunk, step],
                (peer, blk),
            )
            copy.start()
            row.append(copy)
        first.append(row)
    second = []
    for chunk in range(CHUNKS):
        mine[chunk].wait()
        for copy in first[chunk]:
            copy.wait_recv()
        cut = pl.ds(chunk * width, width)
        for step in range(1, owners + 1):
            peer = lax.rem(blk + step, owners)
            source = order[grp, peer] * share
            staged[chunk, peer] = landed[chunk][pl.ds(source, share)]
            if step < owners:
                copy = remote(
                    staged.at[chunk, peer],
                    g.at[:, blk, :, cut],
                    s2.at[chunk, step],
                    r2.at[chunk, step],
                    (grp, peer),
                )
            else:
                copy = pltpu.make_async_copy(
                    staged.at[chunk, blk], g.at[:, blk, :, cut], local2.at[chunk]
                )
            copy.start()
            second.append((copy, step < owners))
    for copy, far in second:
        copy.wait()
    for row in first:
        for copy in row:
            copy.wait_send()


def outbound(groups, owners, order, u, y, landed, staged, local1, local2, s1, r1, s2, r2):
    grp, blk = lax.axis_index("grp"), lax.axis_index("blk")
    share = groups // owners
    width = landed[0].shape[-1]
    block = width * CHUNKS

    def columns(owner, chunk):
        return pl.ds(pl.multiple_of(owner * block + chunk * width, width), width)

    enter(groups, owners, grp, blk)
    first = []
    for chunk in range(CHUNKS):
        row = []
        cut = pl.ds(chunk * width, width)
        for step in range(1, owners):
            peer = lax.rem(blk + step, owners)
            copy = remote(
                u.at[:, peer, :, cut],
                landed[chunk].at[blk],
                s1.at[chunk, step],
                r1.at[chunk, step],
                (grp, peer),
            )
            copy.start()
            row.append(copy)
        copy = pltpu.make_async_copy(
            u.at[:, blk, :, cut], landed[chunk].at[blk], local1.at[chunk]
        )
        copy.start()
        first.append((row, copy))
    places = []
    for position in range(owners):
        place = jnp.int32(0)
        for slot in range(owners):
            place = jnp.where(order[grp, slot] == position, slot, place)
        places.append(place)
    second = []
    for chunk in range(CHUNKS):
        row, copy = first[chunk]
        copy.wait()
        for copy in row:
            copy.wait_recv()
        for position in range(owners):
            for part in range(share):
                staged[chunk, position * share + part] = landed[chunk][places[position], part]
        for step in range(1, groups + 1):
            peer = lax.rem(grp + step, groups)
            if step < groups:
                copy = remote(
                    staged.at[chunk, peer],
                    y.at[:, columns(grp, chunk)],
                    s2.at[chunk, step],
                    r2.at[chunk, step],
                    (peer, blk),
                )
            else:
                copy = pltpu.make_async_copy(
                    staged.at[chunk, grp], y.at[:, columns(grp, chunk)], local2.at[chunk]
                )
            copy.start()
            second.append(copy)
    for copy in second:
        copy.wait()
    for row, copy in first:
        for copy in row:
            copy.wait_send()


def product(left, right):
    return jnp.dot(left.astype(BF16), right.astype(BF16), preferred_element_type=F32)


def local(
    owners,
    picks,
    slots,
    steps,
    g,
    left_old,
    right_old,
    left_stored,
    right_stored,
    left_out,
    right_out,
    left_root,
    right_root,
    u,
    stats,
    roots,
    moving,
    iterate,
    in_sem,
    root_sem,
    out_sem,
    done_sem,
):
    size = g.shape[0]
    loads, root_loads = [], []
    for side, ref in enumerate((left_old, right_old)):
        loads.append(pltpu.make_async_copy(ref, stats.at[side], in_sem.at[side]))
        loads[-1].start()
    for side, ref in enumerate((left_stored, right_stored)):
        root_loads.append(pltpu.make_async_copy(ref, roots.at[side], root_sem.at[side]))
        root_loads[-1].start()
    mine = lax.axis_index("grp") * owners + lax.axis_index("blk")
    count = jnp.int32(0)
    for pick in range(picks):
        count = count + jnp.where(slots[pick] == mine, steps[pick], 0)
    weight = (1.0 - decay_rate) / size
    stores = []
    for side, (dims, ref) in enumerate(((1, left_out), (0, right_out))):
        gram = lax.dot_general(
            g[...], g[...], (((dims,), (dims,)), ((), ())), preferred_element_type=F32
        )
        loads[side].wait()
        stats[side] = decay_rate * stats[side] + weight * gram
        stores.append(pltpu.make_async_copy(stats.at[side], ref, out_sem.at[side]))
        stores[-1].start()
    for copy in root_loads:
        copy.wait()

    lead = (root_order + 1.0) / root_order
    square = lead * lead

    def unit(scale):
        rows = lax.broadcasted_iota(jnp.int32, (size, size), 0)
        cols = lax.broadcasted_iota(jnp.int32, (size, size), 1)
        return jnp.where(rows == cols, jnp.float32(scale), jnp.float32(0.0))

    def advance(m):
        part = product(m, m) / root_order**2 - (2.0 * lead / root_order) * m
        fourth = 2.0 * square * part + product(part, part)
        return square * square * m + product(fourth, m)

    @pl.when(count > 0)
    def refresh():
        scales = []
        for side in range(2):
            shifted = stats[side] + unit(damping)
            frobenius = jnp.sqrt(jnp.full((1, 1), jnp.sum(shifted * shifted), F32))
            scaling = (1.0 + root_order) / (2.0 * frobenius)
            scales.append(jnp.sqrt(jnp.sqrt(scaling)))
            moving[side] = scaling * shifted
            iterate[side] = unit(lead) - moving[side] / root_order

        @pl.when(count > 1)
        def again():
            for side in range(2):
                m = moving[side]
                after = advance(m)
                both = lead * after - product(m, after) / root_order
                moving[side] = after
                iterate[side] = lead * iterate[side] - both / root_order

        @pl.when(count > 2)
        def last():
            for side in range(2):
                y = iterate[side]
                iterate[side] = lead * y - product(y, advance(moving[side])) / root_order

        for side in range(2):
            roots[side] = (scales[side] * iterate[side]).astype(BF16)

    for side, ref in enumerate((left_root, right_root)):
        stores.append(pltpu.make_async_copy(roots.at[side], ref, done_sem.at[side]))
        stores[-1].start()
    half = jnp.dot(g[...], roots[1], preferred_element_type=F32).astype(BF16)
    precon = jnp.dot(roots[0], half, preferred_element_type=F32)
    wide = g[...].astype(F32)
    area = float(size * size)
    top = jnp.full((1, 1), jnp.sum(wide * wide), F32) / area
    bottom = jnp.full((1, 1), jnp.sum(precon * precon), F32) / area
    ratio = jnp.sqrt(top) / jnp.sqrt(bottom + 1e-06)
    u[...] = (precon * ratio).astype(BF16)
    for copy in stores:
        copy.wait()


ANY = pl.BlockSpec(memory_space=pl.ANY)
SMEM = pl.BlockSpec(memory_space=pltpu.SMEM)
VMEM = pl.BlockSpec(memory_space=pltpu.VMEM)
DMA = pltpu.SemaphoreType.DMA


def per_device(
    gradient,
    stats_left,
    stats_right,
    root_left,
    root_right,
    slot_block,
    refresh_slots,
    newton_steps,
):
    groups = lax.axis_size("grp")
    owners = lax.axis_size("blk")
    rows = gradient.shape[0]
    size = stats_left.shape[1]
    share = groups // owners
    width = size // CHUNKS
    g = pl.pallas_call(
        functools.partial(inbound, groups, owners),
        name="inbound",
        out_shape=jax.ShapeDtypeStruct((share, owners, rows, size), BF16),
        in_specs=[SMEM, ANY],
        out_specs=ANY,
        scratch_shapes=[
            [pltpu.VMEM((groups, rows, width), BF16)] * CHUNKS,
            pltpu.VMEM((CHUNKS, owners, share, rows, width), BF16),
            DMA((CHUNKS,)),
            DMA((CHUNKS,)),
            DMA((CHUNKS, groups)),
            DMA((CHUNKS, groups)),
            DMA((CHUNKS, owners)),
            DMA((CHUNKS, owners)),
        ],
        compiler_params=pltpu.CompilerParams(collective_id=0, has_side_effects=True),
    )(slot_block, gradient)
    square = jax.ShapeDtypeStruct((size, size), F32)
    narrow = jax.ShapeDtypeStruct((size, size), BF16)
    left_new, right_new, left_root, right_root, u = pl.pallas_call(
        functools.partial(local, owners, refresh_slots.shape[0]),
        name="local",
        out_shape=(square, square, narrow, narrow, narrow),
        in_specs=[SMEM, SMEM, VMEM, ANY, ANY, ANY, ANY],
        out_specs=(ANY, ANY, ANY, ANY, VMEM),
        scratch_shapes=[
            pltpu.VMEM((2, size, size), F32),
            pltpu.VMEM((2, size, size), BF16),
            pltpu.VMEM((2, size, size), F32),
            pltpu.VMEM((2, size, size), F32),
            DMA((2,)),
            DMA((2,)),
            DMA((2,)),
            DMA((2,)),
        ],
        compiler_params=pltpu.CompilerParams(vmem_limit_bytes=48 * 2**20),
    )(
        refresh_slots,
        newton_steps,
        g.reshape(size, size),
        stats_left[0],
        stats_right[0],
        root_left[0],
        root_right[0],
    )
    y = pl.pallas_call(
        functools.partial(outbound, groups, owners),
        name="outbound",
        out_shape=jax.ShapeDtypeStruct(gradient.shape, BF16),
        in_specs=[SMEM, ANY],
        out_specs=ANY,
        scratch_shapes=[
            [pltpu.VMEM((owners, share, rows, width), BF16)] * CHUNKS,
            pltpu.VMEM((CHUNKS, groups, rows, width), BF16),
            DMA((CHUNKS,)),
            DMA((CHUNKS,)),
            DMA((CHUNKS, owners)),
            DMA((CHUNKS, owners)),
            DMA((CHUNKS, groups)),
            DMA((CHUNKS, groups)),
        ],
        compiler_params=pltpu.CompilerParams(collective_id=1, has_side_effects=True),
    )(slot_block, u.reshape(share, owners, rows, size))
    return (left_new[None], right_new[None], left_root[None], right_root[None], y)


def solution(mesh):
    placed = (
        P(("grp", "blk"), None),
        P(("grp", "blk"), None, None),
        P(("grp", "blk"), None, None),
        P(("grp", "blk"), None, None),
        P(("grp", "blk"), None, None),
        P(),
        P(),
        P(),
    )
    return jax.shard_map(
        per_device,
        mesh=mesh,
        in_specs=placed,
        out_specs=(
            P(("grp", "blk"), None, None),
            P(("grp", "blk"), None, None),
            P(("grp", "blk"), None, None),
            P(("grp", "blk"), None, None),
            P(("grp", "blk"), None),
        ),
        check_vma=False,
    )
```

time: 132 us -> 62.3 us (0.47)
  the two profiles are of different devices: /device:TPU:0 before, /device:TPU:27 now
where the time goes in v1:
time: 62.3 us; the launch traced here: 61.4 us
  Pallas kernels  51.6 us (83%)
  local copies, waits for them, and re-layouts  9.09 us (15%)
  between operations  0.7 us (1%)
    pallas_call x1, Pallas kernels, per_device(): pl.pallas_call(functools.partial(outbound, groups, owners), name='outboun...  25.5 us
    pallas_call x1, Pallas kernels, per_device(): pl.pallas_call(functools.partial(inbound, groups, owners), name='inbound'...  22.6 us
    unnamed x18, local copies, waits for them, and re-layouts  9.09 us
    pallas_call x1, Pallas kernels, per_device(): pl.pallas_call(functools.partial(local, owners, refresh_slots.shape[0]),...  3.58 us

profile of v1, /device:TPU:27, one launch (start us, length us, event | category | flops | bytes accessed | tf_op | source)
XLA Modules:
  0.0 61.4 jit_solution(3331574867845568223)
XLA Ops:
  0.6 0.0 copy-start.1
  0.6 1.4 %copy.13.order = s32[8,4]{1,0:T(8,128)} copy(s32[8,4]{0,1:T(4,128)} %param.13) | data formatting | bytes 256 | tf_op args[5]
  2.1 22.6 %inbound.1 = bf16[2,4,64,512]{3,2,1,0:T(8,128)(2,1)} custom-call(s32[8,4]{1,0:T(8,128)} %copy.13.order, bf16[64,4096]{1,0:T(8,128)(2,1)} %x.1), custom_call_target="tpu_custom_call" | custom-call | tf_op jit(solution)/shard_map/inbound/pallas_call | solution.py:304
  24.6 0.0 copy-start.6
  24.7 0.0 copy-start.7
  24.7 0.0 copy-done.1
  24.7 0.6 %copy-done.6 = s32[4]{0:T(128)S(1)} copy-done((s32[4]{0:T(128)S(1)}, s32[4]{0:T(128)}, u32[]{:S(2)}) %copy-start.6) | copy-done | bytes 40
  25.3 0.0 copy-done.7
  25.3 0.0 copy-start
  25.3 1.0 %copy-done = bf16[2,4,64,512]{3,2,1,0:T(8,128)(2,1)S(1)} copy-done((bf16[2,4,64,512]{3,2,1,0:T(8,128)(2,1)S(1)}, bf16[2,4,64,512]{3,2,1,0:T(8,128)(2,1)}, u32[]{:S(2)}) %copy-start) | copy-done | bytes 524312
  26.4 0.0 copy-start.2
  26.4 1.2 %copy-done.2 = f32[1,512,512]{2,1,0:T(8,128)S(1)} copy-done((f32[1,512,512]{2,1,0:T(8,128)S(1)}, f32[1,512,512]{2,1,0:T(8,128)}, u32[]{:S(2)}) %copy-start.2) | copy-done | bytes 1048600
  27.6 0.0 copy-start.4
  27.6 1.0 %copy-done.4 = bf16[1,512,512]{2,1,0:T(8,128)(2,1)S(1)} copy-done((bf16[1,512,512]{2,1,0:T(8,128)(2,1)S(1)}, bf16[1,512,512]{2,1,0:T(8,128)(2,1)}, u32[]{:S(2)}) %copy-start.4) | copy-done | bytes 524312
  28.6 0.0 copy-start.5
  28.6 1.0 %copy-done.5 = bf16[1,512,512]{2,1,0:T(8,128)(2,1)S(1)} copy-done((bf16[1,512,512]{2,1,0:T(8,128)(2,1)S(1)}, bf16[1,512,512]{2,1,0:T(8,128)(2,1)}, u32[]{:S(2)}) %copy-start.5) | copy-done | bytes 524312
  29.7 3.6 %local.1 = (f32[512,512]{1,0:T(8,128)}, f32[512,512]{1,0:T(8,128)}, bf16[512,512]{1,0:T(8,128)(2,1)}, bf16[512,512]{1,0:T(8,128)(2,1)}, bf16[512,512]{1,0:T(8,128)(2,1)S(1)}) custom-call(s32[4]{0:T(128)S(1)} %copy-done.6, s32[4]{0:T(128)S(1)} %copy-done.7, bf16[512,512]{1,0:T(8,128)(2,1)S(1)} %bitcast.10, f32[512,512]{1,0:T(8,128)S(1)} %bitcast.11, ...), custom_call_target="tpu_custom_call" | custom-call | tf_op jit(solution)/shard_map/local/pallas_call | solution.py:324
  33.3 0.0 copy-start.3
  33.3 0.8 %copy-done.3 = bf16[512,512]{1,0:T(8,128)(2,1)} copy-done((bf16[512,512]{1,0:T(8,128)(2,1)}, bf16[512,512]{1,0:T(8,128)(2,1)S(1)}, u32[]{:S(2)}) %copy-start.3) | copy-done | bytes 524312
  34.1 25.5 %outbound.1 = bf16[64,4096]{1,0:T(8,128)(2,1)} custom-call(s32[8,4]{1,0:T(8,128)} %copy.13.order, bf16[2,4,64,512]{3,2,1,0:T(8,128)(2,1)} %bitcast.13), custom_call_target="tpu_custom_call" | custom-call | tf_op jit(solution)/shard_map/outbound/pallas_call | solution.py:350
  59.5 1.9 %copy.16 = bf16[64,4096]{1,0:T(8,128)(2,1)} copy(bf16[64,4096]{1,0:T(8,128)(2,1)} %outbound.1) | data formatting | bytes 1048576
Async XLA Ops:
  0.6 24.0 %copy-start.1 = (f32[1,512,512]{2,1,0:T(8,128)S(1)}, f32[1,512,512]{2,1,0:T(8,128)}, u32[]{:S(2)}) copy-start(f32[1,512,512]{2,1,0:T(8,128)} %param.9) | copy-start | bytes 3145732
  24.6 0.7 %copy-start.6 = (s32[4]{0:T(128)S(1)}, s32[4]{0:T(128)}, u32[]{:S(2)}) copy-start(s32[4]{0:T(128)} %slots.1) | copy-start | bytes 52
  24.7 0.7 %copy-start.7 = (s32[4]{0:T(128)S(1)}, s32[4]{0:T(128)}, u32[]{:S(2)}) copy-start(s32[4]{0:T(128)} %steps.1) | copy-start | bytes 52
  25.3 1.0 %copy-start = (bf16[2,4,64,512]{3,2,1,0:T(8,128)(2,1)S(1)}, bf16[2,4,64,512]{3,2,1,0:T(8,128)(2,1)}, u32[]{:S(2)}) copy-start(bf16[2,4,64,512]{3,2,1,0:T(8,128)(2,1)} %inbound.1) | copy-start | bytes 1572868
  26.4 1.2 %copy-start.2 = (f32[1,512,512]{2,1,0:T(8,128)S(1)}, f32[1,512,512]{2,1,0:T(8,128)}, u32[]{:S(2)}) copy-start(f32[1,512,512]{2,1,0:T(8,128)} %param.10) | copy-start | bytes 3145732
  27.6 1.0 %copy-start.4 = (bf16[1,512,512]{2,1,0:T(8,128)(2,1)S(1)}, bf16[1,512,512]{2,1,0:T(8,128)(2,1)}, u32[]{:S(2)}) copy-start(bf16[1,512,512]{2,1,0:T(8,128)(2,1)} %param.11) | copy-start | bytes 1572868
  28.6 1.0 %copy-start.5 = (bf16[1,512,512]{2,1,0:T(8,128)(2,1)S(1)}, bf16[1,512,512]{2,1,0:T(8,128)(2,1)}, u32[]{:S(2)}) copy-start(bf16[1,512,512]{2,1,0:T(8,128)(2,1)} %param.12) | copy-start | bytes 1572868
  33.3 0.8 %copy-start.3 = (bf16[512,512]{1,0:T(8,128)(2,1)}, bf16[512,512]{1,0:T(8,128)(2,1)S(1)}, u32[]{:S(2)}) copy-start(bf16[512,512]{1,0:T(8,128)(2,1)S(1)} %get-tuple-element.14) | copy-start | bytes 1572868

commit v2 on v1

--- a/solution.py
+++ b/solution.py
@@ -10,7 +10,10 @@
 damping = 0.0001
 decay_rate = 0.9
 root_order = 4.0
-CHUNKS = 2
+CHUNKS = 4
+GRANT = 28 * 2**20
+SMALL = 12 * 2**20
+WIDE = 12 * 2**20
 MESH = pl.DeviceIdType.MESH
 F32 = jnp.float32
 BF16 = jnp.bfloat16
@@ -38,8 +41,16 @@
     )
 
 
-def inbound(groups, owners, order, x, g, landed, staged, local1, local2, s1, r1, s2, r2):
+def inbound(groups, owners, picks, *refs):
+    table, slots_in, steps_in, x = refs[:4]
+    held_in, held = refs[4:8], refs[10:14]
+    g, info = refs[8:10]
+    order, slots, steps, landed, staged, local1, local2, s1, r1, s2, r2, small, large = refs[14:]
     grp, blk = lax.axis_index("grp"), lax.axis_index("blk")
+    tables = []
+    for place, (source, target) in enumerate(((table, order), (slots_in, slots), (steps_in, steps))):
+        tables.append(pltpu.make_async_copy(source, target, small.at[place]))
+        tables[-1].start()
     share = groups // owners
     block = landed[0].shape[-1] * CHUNKS
     width = landed[0].shape[-1]
@@ -70,6 +81,17 @@
             copy.start()
             row.append(copy)
         first.append(row)
+    loads = []
+    for place in range(4):
+        loads.append(pltpu.make_async_copy(held_in[place], held[place], large.at[place]))
+        loads[-1].start()
+    for copy in tables:
+        copy.wait()
+    own = grp * owners + blk
+    count = jnp.int32(0)
+    for pick in range(picks):
+        count = count + jnp.where(slots[pick] == own, steps[pick], 0)
+    info[...] = jnp.full(info.shape, count, jnp.int32)
     second = []
     for chunk in range(CHUNKS):
         mine[chunk].wait()
@@ -78,7 +100,7 @@
         cut = pl.ds(chunk * width, width)
         for step in range(1, owners + 1):
             peer = lax.rem(blk + step, owners)
-            source = order[grp, peer] * share
+            source = order[peer, grp] * share
             staged[chunk, peer] = landed[chunk][pl.ds(source, share)]
             if step < owners:
                 copy = remote(
@@ -93,16 +115,22 @@
                     staged.at[chunk, blk], g.at[:, blk, :, cut], local2.at[chunk]
                 )
             copy.start()
-            second.append((copy, step < owners))
-    for copy, far in second:
+            second.append(copy)
+    for copy in second:
+        copy.wait()
+    for copy in loads:
         copy.wait()
     for row in first:
         for copy in row:
             copy.wait_send()
 
 
-def outbound(groups, owners, order, u, y, landed, staged, local1, local2, s1, r1, s2, r2):
+def outbound(
+    groups, owners, table, u, y, order, landed, staged, local1, local2, s1, r1, s2, r2, small
+):
     grp, blk = lax.axis_index("grp"), lax.axis_index("blk")
+    fetch = pltpu.make_async_copy(table, order, small)
+    fetch.start()
     share = groups // owners
     width = landed[0].shape[-1]
     block = width * CHUNKS
@@ -131,11 +159,12 @@
         )
         copy.start()
         first.append((row, copy))
+    fetch.wait()
     places = []
     for position in range(owners):
         place = jnp.int32(0)
         for slot in range(owners):
-            place = jnp.where(order[grp, slot] == position, slot, place)
+            place = jnp.where(order[slot, grp] == position, slot, place)
         places.append(place)
     second = []
     for chunk in range(CHUNKS):
@@ -174,10 +203,7 @@
 
 
 def local(
-    owners,
-    picks,
-    slots,
-    steps,
+    info,
     g,
     left_old,
     right_old,
@@ -192,35 +218,22 @@
     roots,
     moving,
     iterate,
-    in_sem,
-    root_sem,
     out_sem,
     done_sem,
 ):
     size = g.shape[0]
-    loads, root_loads = [], []
-    for side, ref in enumerate((left_old, right_old)):
-        loads.append(pltpu.make_async_copy(ref, stats.at[side], in_sem.at[side]))
-        loads[-1].start()
-    for side, ref in enumerate((left_stored, right_stored)):
-        root_loads.append(pltpu.make_async_copy(ref, roots.at[side], root_sem.at[side]))
-        root_loads[-1].start()
-    mine = lax.axis_index("grp") * owners + lax.axis_index("blk")
-    count = jnp.int32(0)
-    for pick in range(picks):
-        count = count + jnp.where(slots[pick] == mine, steps[pick], 0)
+    count = jnp.max(info[...])
     weight = (1.0 - decay_rate) / size
     stores = []
-    for side, (dims, ref) in enumerate(((1, left_out), (0, right_out))):
+    for side, (dims, old, ref) in enumerate(((1, left_old, left_out), (0, right_old, right_out))):
         gram = lax.dot_general(
             g[...], g[...], (((dims,), (dims,)), ((), ())), preferred_element_type=F32
         )
-        loads[side].wait()
-        stats[side] = decay_rate * stats[side] + weight * gram
+        stats[side] = decay_rate * old[...] + weight * gram
         stores.append(pltpu.make_async_copy(stats.at[side], ref, out_sem.at[side]))
         stores[-1].start()
-    for copy in root_loads:
-        copy.wait()
+    roots[0] = left_stored[...]
+    roots[1] = right_stored[...]
 
     lead = (root_order + 1.0) / root_order
     square = lead * lead
@@ -279,8 +292,7 @@
         copy.wait()
 
 
-ANY = pl.BlockSpec(memory_space=pl.ANY)
-SMEM = pl.BlockSpec(memory_space=pltpu.SMEM)
+HBM = pl.BlockSpec(memory_space=pltpu.HBM)
 VMEM = pl.BlockSpec(memory_space=pltpu.VMEM)
 DMA = pltpu.SemaphoreType.DMA
 
@@ -301,13 +313,27 @@
     size = stats_left.shape[1]
     share = groups // owners
     width = size // CHUNKS
-    g = pl.pallas_call(
-        functools.partial(inbound, groups, owners),
+    square = jax.ShapeDtypeStruct((size, size), F32)
+    narrow = jax.ShapeDtypeStruct((size, size), BF16)
+    picks = refresh_slots.shape[0]
+    table = slot_block.T
+    g, info, *held = pl.pallas_call(
+        functools.partial(inbound, groups, owners, picks),
         name="inbound",
-        out_shape=jax.ShapeDtypeStruct((share, owners, rows, size), BF16),
-        in_specs=[SMEM, ANY],
-        out_specs=ANY,
+        out_shape=(
+            jax.ShapeDtypeStruct((share, owners, rows, size), BF16),
+            jax.ShapeDtypeStruct((8, 128), jnp.int32),
+            square,
+            square,
+            narrow,
+            narrow,
+        ),
+        in_specs=[HBM] * 8,
+        out_specs=(VMEM,) * 6,
         scratch_shapes=[
+            pltpu.SMEM(table.shape, jnp.int32),
+            pltpu.SMEM((picks,), jnp.int32),
+            pltpu.SMEM((picks,), jnp.int32),
             [pltpu.VMEM((groups, rows, width), BF16)] * CHUNKS,
             pltpu.VMEM((CHUNKS, owners, share, rows, width), BF16),
             DMA((CHUNKS,)),
@@ -316,17 +342,33 @@
             DMA((CHUNKS, groups)),
             DMA((CHUNKS, owners)),
             DMA((CHUNKS, owners)),
+            DMA((3,)),
+            DMA((4,)),
         ],
-        compiler_params=pltpu.CompilerParams(collective_id=0, has_side_effects=True),
-    )(slot_block, gradient)
-    square = jax.ShapeDtypeStruct((size, size), F32)
-    narrow = jax.ShapeDtypeStruct((size, size), BF16)
+        compiler_params=pltpu.CompilerParams(
+            collective_id=0, has_side_effects=True, vmem_limit_bytes=WIDE
+        ),
+    )(
+        *(
+            pltpu.with_memory_space_constraint(array, pltpu.HBM)
+            for array in (
+                table,
+                refresh_slots,
+                newton_steps,
+                gradient,
+                stats_left[0],
+                stats_right[0],
+                root_left[0],
+                root_right[0],
+            )
+        )
+    )
     left_new, right_new, left_root, right_root, u = pl.pallas_call(
-        functools.partial(local, owners, refresh_slots.shape[0]),
+        local,
         name="local",
         out_shape=(square, square, narrow, narrow, narrow),
-        in_specs=[SMEM, SMEM, VMEM, ANY, ANY, ANY, ANY],
-        out_specs=(ANY, ANY, ANY, ANY, VMEM),
+        in_specs=[VMEM] * 6,
+        out_specs=(HBM, HBM, HBM, HBM, VMEM),
         scratch_shapes=[
             pltpu.VMEM((2, size, size), F32),
             pltpu.VMEM((2, size, size), BF16),
@@ -334,26 +376,17 @@
             pltpu.VMEM((2, size, size), F32),
             DMA((2,)),
             DMA((2,)),
-            DMA((2,)),
-            DMA((2,)),
         ],
-        compiler_params=pltpu.CompilerParams(vmem_limit_bytes=48 * 2**20),
-    )(
-        refresh_slots,
-        newton_steps,
-        g.reshape(size, size),
-        stats_left[0],
-        stats_right[0],
-        root_left[0],
-        root_right[0],
-    )
+        compiler_params=pltpu.CompilerParams(vmem_limit_bytes=GRANT),
+    )(info, g.reshape(size, size), *held)
     y = pl.pallas_call(
         functools.partial(outbound, groups, owners),
         name="outbound",
         out_shape=jax.ShapeDtypeStruct(gradient.shape, BF16),
-        in_specs=[SMEM, ANY],
-        out_specs=ANY,
+        in_specs=[HBM, VMEM],
+        out_specs=VMEM,
         scratch_shapes=[
+            pltpu.SMEM(table.shape, jnp.int32),
             [pltpu.VMEM((owners, share, rows, width), BF16)] * CHUNKS,
             pltpu.VMEM((CHUNKS, groups, rows, width), BF16),
             DMA((CHUNKS,)),
@@ -362,9 +395,12 @@
             DMA((CHUNKS, owners)),
             DMA((CHUNKS, groups)),
             DMA((CHUNKS, groups)),
+            DMA,
         ],
-        compiler_params=pltpu.CompilerParams(collective_id=1, has_side_effects=True),
-    )(slot_block, u.reshape(share, owners, rows, size))
+        compiler_params=pltpu.CompilerParams(
+            collective_id=1, has_side_effects=True, vmem_limit_bytes=SMALL
+        ),
+    )(pltpu.with_memory_space_constraint(table, pltpu.HBM), u.reshape(share, owners, rows, size))
     return (left_new[None], right_new[None], left_root[None], right_root[None], y)
 
 

time: 62.3 us -> 49.9 us (0.80)
  the two profiles are of different devices: /device:TPU:27 before, /device:TPU:0 now
where the time goes in v2:
time: 49.9 us; the launch traced here: 49.1 us
  Pallas kernels  47.7 us (96%)
  local copies, waits for them, and re-layouts  0.8 us (2%)
  between operations  0.66 us (1%)
    pallas_call x1, Pallas kernels, per_device(): pl.pallas_call(functools.partial(inbound, groups, owners, picks), name='i...  23.5 us
    pallas_call x1, Pallas kernels, per_device(): pl.pallas_call(functools.partial(outbound, groups, owners), name='outboun...  21.1 us
    pallas_call x1, Pallas kernels, per_device(): pl.pallas_call(local, name='local', out_shape=(square, square, narrow, na...  3.07 us

profile of v2, /device:TPU:0, one launch (start us, length us, event | category | flops | bytes accessed | tf_op | source)
XLA Modules:
  0.0 49.1 jit_solution(10326767168429045986)
XLA Ops:
  0.6 23.5 %inbound.1 = (bf16[2,4,64,512]{3,2,1,0:T(8,128)(2,1)S(1)}, s32[8,128]{1,0:T(8,128)S(1)}, f32[512,512]{1,0:T(8,128)S(1)}, f32[512,512]{1,0:T(8,128)S(1)}, bf16[51...) custom-call(s32[4,8]{1,0:T(4,128)} %bitcast.17, s32[4]{0:T(128)} %refs_1_.1, s32[4]{0:T(128)} %refs_2_.1, ...), custom_call_target="tpu_custom_call" | custom-call | tf_op jit(solution)/shard_map/inbound/pallas_call | solution.py:320
  24.2 3.1 %local.1 = (f32[512,512]{1,0:T(8,128)}, f32[512,512]{1,0:T(8,128)}, bf16[512,512]{1,0:T(8,128)(2,1)}, bf16[512,512]{1,0:T(8,128)(2,1)}, bf16[512,512]{1,0:T(8,128)(2,1)S(1)}) custom-call(s32[8,128]{1,0:T(8,128)S(1)} %get-tuple-element.16.info, bf16[512,512]{1,0:T(8,128)(2,1)S(1)} %bitcast.12, f32[512,512]{1,0:T(8,128)S(1)} %get-tuple-element.18.left_old, ...), custom_call_target="tpu_custom_call" | custom-call | tf_op jit(solution)/shard_map/local/pallas_call | solution.py:366
  27.2 21.1 %outbound.1 = bf16[64,4096]{1,0:T(8,128)(2,1)S(1)} custom-call(s32[4,8]{1,0:T(4,128)} %bitcast.18, bf16[2,4,64,512]{3,2,1,0:T(8,128)(2,1)S(1)} %bitcast.11), custom_call_target="tpu_custom_call" | custom-call | tf_op jit(solution)/shard_map/outbound/pallas_call | solution.py:382
  48.3 0.8 %copy.14 = bf16[64,4096]{1,0:T(8,128)(2,1)} copy(bf16[64,4096]{1,0:T(8,128)(2,1)S(1)} %outbound.1) | data formatting | bytes 1048576

commit v3 on v2

--- a/solution.py
+++ b/solution.py
@@ -92,32 +92,46 @@
     for pick in range(picks):
         count = count + jnp.where(slots[pick] == own, steps[pick], 0)
     info[...] = jnp.full(info.shape, count, jnp.int32)
-    second = []
+    second, arriving = [], []
     for chunk in range(CHUNKS):
         mine[chunk].wait()
         for copy in first[chunk]:
             copy.wait_recv()
         cut = pl.ds(chunk * width, width)
-        for step in range(1, owners + 1):
-            peer = lax.rem(blk + step, owners)
+        for place in range(owners):
+            peer = far_first(owners, blk, place) if place < owners - 1 else blk
             source = order[peer, grp] * share
             staged[chunk, peer] = landed[chunk][pl.ds(source, share)]
-            if step < owners:
+            if place < owners - 1:
                 copy = remote(
                     staged.at[chunk, peer],
                     g.at[:, blk, :, cut],
-                    s2.at[chunk, step],
-                    r2.at[chunk, step],
+                    s2.at[chunk, peer],
+                    r2.at[chunk, blk],
                     (grp, peer),
+                )
+                arriving.append(
+                    remote(
+                        staged.at[chunk, peer],
+                        g.at[:, peer, :, cut],
+                        s2.at[chunk, peer],
+                        r2.at[chunk, peer],
+                        (grp, peer),
+                    )
                 )
             else:
                 copy = pltpu.make_async_copy(
                     staged.at[chunk, blk], g.at[:, blk, :, cut], local2.at[chunk]
                 )
             copy.start()
-            second.append(copy)
-    for copy in second:
-        copy.wait()
+            second.append((copy, place < owners - 1))
+    for copy, far in second:
+        if far:
+            copy.wait_send()
+        else:
+            copy.wait()
+    for copy in arriving:
+        copy.wait_recv()
     for copy in loads:
         copy.wait()
     for row in first:
@@ -143,17 +157,15 @@
     for chunk in range(CHUNKS):
         row = []
         cut = pl.ds(chunk * width, width)
-        for step in range(1, owners):
-            peer = lax.rem(blk + step, owners)
-            copy = remote(
-                u.at[:, peer, :, cut],
-                landed[chunk].at[blk],
-                s1.at[chunk, step],
-                r1.at[chunk, step],
-                (grp, peer),
+        for place in range(owners - 1):
+            peer = far_first(owners, blk, place)
+            source = u.at[:, peer, :, cut]
+            send = s1.at[chunk, peer]
+            copy = remote(source, landed[chunk].at[blk], send, r1.at[chunk, blk], (grp, peer))
+            copy.start()
+            row.append(
+                remote(source, landed[chunk].at[peer], send, r1.at[chunk, peer], (grp, peer))
             )
-            copy.start()
-            row.append(copy)
         copy = pltpu.make_async_copy(
             u.at[:, blk, :, cut], landed[chunk].at[blk], local1.at[chunk]
         )
@@ -198,6 +210,22 @@
             copy.wait_send()
 
 
+def far_first(owners, blk, place):
+    falling = owners - 1 - place
+    falling = falling - jnp.where(falling <= blk, 1, 0)
+    rising = place + jnp.where(place >= blk, 1, 0)
+    return jnp.where(blk < owners // 2, falling, rising)
+
+
+def commuting(left, right):
+    left, right = left.astype(BF16), right.astype(BF16)
+    half = left.shape[0] // 2
+    top = jnp.dot(left[:half], right, preferred_element_type=F32)
+    corner = jnp.dot(left[half:], right[:, half:], preferred_element_type=F32)
+    bottom = jnp.concatenate([top[:, half:].T, corner], axis=1)
+    return jnp.concatenate([top, bottom], axis=0)
+
+
 def product(left, right):
     return jnp.dot(left.astype(BF16), right.astype(BF16), preferred_element_type=F32)
 
@@ -244,9 +272,9 @@
         return jnp.where(rows == cols, jnp.float32(scale), jnp.float32(0.0))
 
     def advance(m):
-        part = product(m, m) / root_order**2 - (2.0 * lead / root_order) * m
-        fourth = 2.0 * square * part + product(part, part)
-        return square * square * m + product(fourth, m)
+        part = commuting(m, m) / root_order**2 - (2.0 * lead / root_order) * m
+        fourth = 2.0 * square * part + commuting(part, part)
+        return square * square * m + commuting(fourth, m)
 
     @pl.when(count > 0)
     def refresh():
@@ -264,7 +292,7 @@
             for side in range(2):
                 m = moving[side]
                 after = advance(m)
-                both = lead * after - product(m, after) / root_order
+                both = lead * after - commuting(m, after) / root_order
                 moving[side] = after
                 iterate[side] = lead * iterate[side] - both / root_order
 
@@ -272,7 +300,7 @@
         def last():
             for side in range(2):
                 y = iterate[side]
-                iterate[side] = lead * y - product(y, advance(moving[side])) / root_order
+                iterate[side] = lead * y - commuting(y, advance(moving[side])) / root_order
 
         for side in range(2):
             roots[side] = (scales[side] * iterate[side]).astype(BF16)

time: 49.9 us -> 48.6 us (0.974)
  Pallas kernels: 47.7 us -> 46.8 us
    pallas_call x1, Pallas kernels: 21.1 us -> 17.7 us  [per_device(): pl.pallas_call(functools.partial(outbound, groups, owners), name='outboun...]
    pallas_call x1, Pallas kernels: 3.07 us -> 5.61 us  [per_device(): pl.pallas_call(local, name='local', out_shape=(square, square, narrow, na...]
where the time goes in v3:
time: 48.6 us; the launch traced here: 48.3 us
  Pallas kernels  46.8 us (96%)
  local copies, waits for them, and re-layouts  0.8 us (2%)
  between operations  0.66 us (1%)
    pallas_call x1, Pallas kernels, per_device(): pl.pallas_call(functools.partial(inbound, groups, owners, picks), name='i...  23.5 us
    pallas_call x1, Pallas kernels, per_device(): pl.pallas_call(functools.partial(outbound, groups, owners), name='outboun...  17.7 us
    pallas_call x1, Pallas kernels, per_device(): pl.pallas_call(local, name='local', out_shape=(square, square, narrow, na...  5.61 us

profile of v3, /device:TPU:0, one launch (start us, length us, event | category | flops | bytes accessed | tf_op | source)
XLA Modules:
  0.0 48.3 jit_solution(3276795486347307014)
XLA Ops:
  0.6 23.5 %inbound.1 = (bf16[2,4,64,512]{3,2,1,0:T(8,128)(2,1)S(1)}, s32[8,128]{1,0:T(8,128)S(1)}, f32[512,512]{1,0:T(8,128)S(1)}, f32[512,512]{1,0:T(8,128)S(1)}, bf16[51...) custom-call(s32[4,8]{1,0:T(4,128)} %bitcast.17, s32[4]{0:T(128)} %refs_1_.1, s32[4]{0:T(128)} %refs_2_.1, ...), custom_call_target="tpu_custom_call" | custom-call | tf_op jit(solution)/shard_map/inbound/pallas_call | solution.py:348
  24.1 5.6 %local.1 = (f32[512,512]{1,0:T(8,128)}, f32[512,512]{1,0:T(8,128)}, bf16[512,512]{1,0:T(8,128)(2,1)}, bf16[512,512]{1,0:T(8,128)(2,1)}, bf16[512,512]{1,0:T(8,128)(2,1)S(1)}) custom-call(s32[8,128]{1,0:T(8,128)S(1)} %get-tuple-element.16.info, bf16[512,512]{1,0:T(8,128)(2,1)S(1)} %bitcast.12, f32[512,512]{1,0:T(8,128)S(1)} %get-tuple-element.18.left_old, ...), custom_call_target="tpu_custom_call" | custom-call | tf_op jit(solution)/shard_map/local/pallas_call | solution.py:394
  29.8 17.7 %outbound.1 = bf16[64,4096]{1,0:T(8,128)(2,1)S(1)} custom-call(s32[4,8]{1,0:T(4,128)} %bitcast.18, bf16[2,4,64,512]{3,2,1,0:T(8,128)(2,1)S(1)} %bitcast.11), custom_call_target="tpu_custom_call" | custom-call | tf_op jit(solution)/shard_map/outbound/pallas_call | solution.py:410
  47.5 0.8 %copy.14 = bf16[64,4096]{1,0:T(8,128)(2,1)} copy(bf16[64,4096]{1,0:T(8,128)(2,1)S(1)} %outbound.1) | data formatting | bytes 1048576
